TPU v7x, 32 devices: a whole 2x2x4 slice. The times are simulated.
32 devices in a mesh: dp: 16 (over z, x, core), fac: 2 (over y).
Axes of the slice: x: 2, y: 2, z: 4, core: 2. Of those that a mesh axis runs over, the one named last changes fastest.
Arguments:
- occupations: int32 [32, 256], P('dp'), may hold values from 0 to 1, as said below
- stream: bfloat16 [8192, 2048], P('dp', 'fac'), may hold values from -6 to 6
- norm_gain: float32 [2048], replicated, may hold values from 0.1 to 1.9
- probs: bfloat16 [32, 16, 256, 256], P('dp', 'fac'), may hold values from 0 to 1, as said below
- w_out: bfloat16 [2048, 2048], P('fac', 'dp'), may hold values from -0.125 to 0.125
- cotangent: bfloat16 [8192, 2048], P('dp', 'fac'), may hold values from -6 to 6
Outputs:
- update: float32 [2048, 2048], P('dp', 'fac')
Inputs may be any that keep to these rules, and one draw needn't show every extreme that they name: `occupations`: each sample holds exactly 48 ones. `probs`: within each sample and head, entries with the key after the query are zero and each row sums to one up to bfloat16 rounding.
All inputs are finite; a program needn't handle non-finite values.
Results may differ from a plain program's by a relative error of at most 0.0051.
Values may be sent and summed in bfloat16 or wider, within the bound.
No kernel may reach another device: no remote copies, remote signals or barrier semaphores. Data moves between devices by JAX's collectives and lax.ppermute only.
A program may use at most 128 MiB of HBM per device.

v0:
```python
import jax
import jax.numpy as jnp
from jax import lax
from jax.sharding import PartitionSpec as P

ORBS = 256
NE = 48
damping = 0.1
epsilon = 1e-06
highest = lax.Precision.HIGHEST
contract_first = (((0,), (0,)), ((), ()))


def keep_mask(occupations):
    before = jnp.cumsum(occupations, axis=1) - occupations
    position = lax.broadcasted_iota(jnp.int32, occupations.shape, 1)
    forced = (before == NE) | (position - before == ORBS - NE)
    return 1 - forced.astype(jnp.int32)


def panel_rows(block):
    return lax.all_gather(block, "fac", axis=2, tiled=True)


def panel_product(left_rows, right_block):
    return jnp.einsum(
        "brk,bkc->brc",
        left_rows,
        lax.all_gather(right_block, "dp", axis=1, tiled=True),
        precision=highest,
    )


def per_device(occupations, stream, norm_gain, probs, w_out, cotangent):
    width = norm_gain.shape[0]
    samples = occupations.shape[0]
    tokens = samples * ORBS
    data_count = lax.axis_size("dp")
    fac_count = lax.axis_size("fac")
    block_rows = width // data_count
    block_cols = width // fac_count
    data_index = lax.axis_index("dp")
    fac_index = lax.axis_index("fac")
    scale = 1.0 / (tokens * data_count)
    stream_whole, cotangent_whole = (
        lax.all_gather(stream, "fac", axis=1, tiled=True),
        lax.all_gather(cotangent, "fac", axis=1, tiled=True),
    )
    values = stream_whole.astype(jnp.float32)
    mean_square = jnp.mean(values * values, axis=1, keepdims=True)
    normed = (values * lax.rsqrt(mean_square + epsilon) * norm_gain).astype(jnp.bfloat16)
    normed_cols = lax.dynamic_slice_in_dim(normed, fac_index * block_cols, block_cols, 1)
    keep = keep_mask(occupations).reshape(tokens, 1).astype(jnp.bfloat16)
    upstream = cotangent_whole * keep
    out_grad = lax.dot_general(
        upstream,
        lax.all_gather(w_out, "dp", axis=1, tiled=True),
        (((1,), (1,)), ((), ())),
        preferred_element_type=jnp.float32,
    ).astype(jnp.bfloat16)
    local_heads = probs.shape[1]
    head_width = block_cols // local_heads
    per_head = out_grad.reshape(samples, ORBS, local_heads, head_width)
    value_local = jnp.einsum("shij,sihe->sjhe", probs, per_head, preferred_element_type=jnp.float32)
    value_local = value_local.reshape(tokens, block_cols).astype(jnp.bfloat16)
    value_whole = lax.all_gather(value_local, "fac", axis=1, tiled=True)
    g_part = (
        lax.dot_general(
            value_whole, value_local, contract_first, preferred_element_type=jnp.float32
        )
        * scale
    )
    grad_part = (
        lax.dot_general(normed, value_local, contract_first, preferred_element_type=jnp.float32)
        * scale
    )
    a_part = (
        lax.dot_general(normed, normed_cols, contract_first, preferred_element_type=jnp.float32)
        * scale
    )
    a_block, g_block, grad_block = (
        lax.psum_scatter(a_part, "dp", scatter_dimension=0, tiled=True),
        lax.psum_scatter(g_part, "dp", scatter_dimension=0, tiled=True),
        lax.psum_scatter(grad_part, "dp", scatter_dimension=0, tiled=True),
    )
    row_ids = data_index * block_rows + lax.broadcasted_iota(jnp.int32, (block_rows, block_cols), 0)
    col_ids = fac_index * block_cols + lax.broadcasted_iota(jnp.int32, (block_rows, block_cols), 1)
    identity_block = (row_ids == col_ids).astype(jnp.float32)
    a_block = a_block + damping * identity_block
    g_block = g_block + damping * identity_block
    norm_a, norm_g = lax.psum(
        (jnp.sum(a_block * a_block), jnp.sum(g_block * g_block)), ("dp", "fac")
    )
    alphas = (1.0 / jnp.sqrt(jnp.stack([norm_a, norm_g]))).reshape(2, 1, 1)
    factors = jnp.stack([a_block, g_block])
    iterate = 2.0 * alphas * identity_block[None] - alphas * alphas * factors
    columns = lax.all_gather(iterate, "dp", axis=1, tiled=True)
    product = jnp.einsum("brk,bkc->brc", panel_rows(factors), columns, precision=highest)
    iterate = 2.0 * iterate - jnp.einsum(
        "brk,bkc->brc", panel_rows(product), columns, precision=highest
    )
    left_side = panel_product(panel_rows(iterate[0:1]), grad_block[None])
    pre = panel_product(panel_rows(left_side), iterate[1:2])[0]
    inner_sum = lax.psum(jnp.sum(grad_block * pre), ("dp", "fac"))
    return pre * (width / jnp.sqrt(inner_sum + epsilon))


def solution(mesh):
    placed = (
        P("dp", None),
        P("dp", "fac"),
        P(),
        P("dp", "fac", None, None),
        P("fac", "dp"),
        P("dp", "fac"),
    )
    return jax.shard_map(
        per_device, mesh=mesh, in_specs=placed, out_specs=P("dp", "fac"), check_vma=False
    )
```

profile of v0, /device:TPU:0, one launch (start us, length us, event | category | flops | bytes accessed | tf_op | source)
XLA Modules:
  0.0 988.1 jit_solution(5292536521925925867)
XLA Ops:
  11.3 33.5 %all-gather.16.cloned.1.call-done = bf16[512,2048]{1,0:T(8,128)(2,1)} async-done(((bf16[512,1024]{1,0:T(8,128)(2,1)}), bf16[512,2048]{1,0:T(8,128)(2,1)}) %all-gather.16.cloned.1.call-update) | async-done | bytes 2097168 | tf_op jit(solution)/shard_map/all_gather | solution.py:47
  44.7 54.7 %all-gather.18.cloned.1.call-done = bf16[1024,2048]{1,0:T(8,128)(2,1)} async-done(((bf16[1024,128]{1,0:T(8,128)(2,1)}), bf16[1024,2048]{1,0:T(8,128)(2,1)}) %all-gather.18.cloned.1.call-update) | async-done | bytes 4194320 | tf_op jit(solution)/shard_map/all_gather | solution.py:57
  99.4 5.2 fusion.11
  106.2 1.3 copy.26
  107.5 24.7 %all-gather.14.cloned.1.call-done = bf16[512,2048]{1,0:T(8,128)(2,1)} async-done(((bf16[512,1024]{1,0:T(8,128)(2,1)}), bf16[512,2048]{1,0:T(8,128)(2,1)}) %all-gather.14.cloned.1.call-update) | async-done | bytes 2097168 | tf_op jit(solution)/shard_map/all_gather | solution.py:46
  132.3 2.1 fusion.2
  134.4 2.1 fusion.4
  136.5 1.3 copy-done.3
  137.8 5.8 convolution_multiply_fusion.2
  143.7 23.0 %all-gather.20.cloned.1.call-done = bf16[512,2048]{1,0:T(8,128)(2,1)} async-done(((bf16[512,1024]{1,0:T(8,128)(2,1)}), bf16[512,2048]{1,0:T(8,128)(2,1)}) %all-gather.20.cloned.1.call-update) | async-done | bytes 2097168 | tf_op jit(solution)/shard_map/all_gather | solution.py:66
  166.8 7.2 convolution_multiply_fusion.1
  174.2 100.0 %reduce-scatter.4.cloned.1.call-done = f32[128,1024]{1,0:T(8,128)} async-done(((f32[2048,1024]{1,0:T(8,128)}), f32[128,1024]{1,0:T(8,128)}) %reduce-scatter.4.cloned.1.call-update) | async-done | bytes 524304 | tf_op jit(solution)/shard_map/reduce_scatter | solution.py:82
  274.1 107.1 %reduce-scatter.6.cloned.1.call-done = f32[128,1024]{1,0:T(8,128)} async-done(((f32[2048,1024]{1,0:T(8,128)}), f32[128,1024]{1,0:T(8,128)}) %reduce-scatter.6.cloned.1.call-update) | async-done | bytes 524304 | tf_op jit(solution)/shard_map/reduce_scatter | solution.py:83
  381.2 2.1 multiply_reduce_fusion.2
  383.3 40.5 %all-reduce = (f32[1]{0:T(128)}, f32[1]{0:T(128)}) all-reduce(f32[1]{0:T(128)} %bitcast.2, f32[1]{0:T(128)} %bitcast), channel_id=1, replica_groups=mesh['dp'=16,'fac'=2] {'dp','fac'}, use_global_device_ids=true, to_apply=%region_8.9 | all-reduce | flops 2 | bytes 16 | tf_op jit(solution)/shard_map/psum | solution.py:91
  423.9 1.3 broadcast_multiply_fusion.1
  425.2 1.5 multiply_subtract_fusion
  427.6 7.5 convolution_multiply_fusion
  435.3 24.2 %all-gather.22.cloned.1.call-done = f32[2,128,2048]{2,1,0:T(8,128)} async-done(((f32[2,128,1024]{2,1,0:T(8,128)}), f32[2,128,2048]{2,1,0:T(8,128)}) %all-gather.22.cloned.1.call-update) | async-done | bytes 2097168 | tf_op jit(solution)/shard_map/all_gather | solution.py:22
  459.5 128.7 %all-gather.24.cloned.1.call-done = f32[2,2048,1024]{2,1,0:T(8,128)} async-done(((f32[2,128,1024]{2,1,0:T(8,128)}), f32[2,2048,1024]{2,1,0:T(8,128)}) %all-gather.24.cloned.1.call-update) | async-done | bytes 16777232 | tf_op jit(solution)/shard_map/all_gather | solution.py:97
  588.1 14.4 %fusion.27 = f32[2,128,1024]{2,1,0:T(8,128)} fusion(f32[2,128,2048]{2,1,0:T(8,128)} %all-gather.22.cloned.1.call-done, f32[2,2048,1024]{2,1,0:T(8,128)} %all-gather.24.cloned.1.call-done), kind=kOutput, calls=%fused_computation.49 | convolution fusion | flops 6442450944 | bytes 19922944 | tf_op jit(solution)/shard_map/brk,bkc->brc/dot_general | solution.py:98
  602.6 91.3 %reduce-scatter.8.cloned.1.call-done = f32[128,1024]{1,0:T(8,128)} async-done(((f32[2048,1024]{1,0:T(8,128)}), f32[128,1024]{1,0:T(8,128)}) %reduce-scatter.8.cloned.1.call-update) | async-done | bytes 524304 | tf_op jit(solution)/shard_map/reduce_scatter | solution.py:84
  693.9 34.1 %all-gather.26.cloned.1.call-done = f32[2,128,2048]{2,1,0:T(8,128)} async-done(((f32[2,128,1024]{2,1,0:T(8,128)}), f32[2,128,2048]{2,1,0:T(8,128)}) %all-gather.26.cloned.1.call-update) | async-done | bytes 2097168 | tf_op jit(solution)/shard_map/all_gather | solution.py:22
  728.0 13.7 %convolution_subtract_fusion = f32[2,128,1024]{2,1,0:T(8,128)S(1)} fusion(f32[2,128,2048]{2,1,0:T(8,128)} %all-gather.26.cloned.1.call-done, f32[2,2048,1024]{2,1,0:T(8,128)} %all-gather.24.cloned.1.call-done, f32[2,128,1024]{2,1,0:T(8,128)S(1)} %copy-done.2), kind=kOutput, calls=%fused_computation.16 | convolution fusion | flops 6442975232 | bytes 20971520 | tf_op jit(solution)/shard_map/brk,bkc->brc/dot_general | solution.py:99
  741.7 1.1 fusion.26
  743.1 61.4 %all-gather.32.cloned.1.call-done = f32[2048,1024]{1,0:T(8,128)} async-done(((f32[128,1024]{1,0:T(8,128)}), f32[2048,1024]{1,0:T(8,128)}) %all-gather.32.cloned.1.call-update) | async-done | bytes 8388624 | tf_op jit(solution)/shard_map/all_gather | solution.py:29
  804.5 21.3 %all-gather.28.cloned.1.call-done = f32[1,128,2048]{2,1,0:T(8,128)} async-done(((f32[1,128,1024]{2,1,0:T(8,128)}), f32[1,128,2048]{2,1,0:T(8,128)}) %all-gather.28.cloned.1.call-update) | async-done | bytes 1048592 | tf_op jit(solution)/shard_map/all_gather | solution.py:22
  825.8 9.2 fusion.14
  835.6 20.8 %all-gather.34.cloned.1.call-done = f32[128,2048]{1,0:T(8,128)} async-done(((f32[128,1024]{1,0:T(8,128)}), f32[128,2048]{1,0:T(8,128)}) %all-gather.34.cloned.1.call-update) | async-done | bytes 1048592 | tf_op jit(solution)/shard_map/all_gather | solution.py:22
  856.4 76.3 %all-gather.30.cloned.1.call-done = f32[1,2048,1024]{2,1,0:T(8,128)} async-done(((f32[1,128,1024]{2,1,0:T(8,128)}), f32[1,2048,1024]{2,1,0:T(8,128)}) %all-gather.30.cloned.1.call-update) | async-done | bytes 8388624 | tf_op jit(solution)/shard_map/all_gather | solution.py:29
  932.8 8.2 multiply_reduce_fusion
  940.9 39.1 %psum.23 = f32[]{:T(128)} all-reduce(f32[]{:T(128)} %get-tuple-element.15), channel_id=1, replica_groups=mesh['dp'=16,'fac'=2] {'dp','fac'}, use_global_device_ids=true, to_apply=%region_11.12 | all-reduce | flops 1 | bytes 8 | tf_op jit(solution)/shard_map/psum | solution.py:104
  (54 shorter events, 9.4 us)
Async XLA Ops:
  6.5 98.3 %copy-start = (bf16[2,8,256,256]{3,2,1,0:T(8,128)(2,1)S(1)}, bf16[2,8,256,256]{3,2,1,0:T(8,128)(2,1)}, u32[]{:S(2)}) copy-start(bf16[2,8,256,256]{3,2,1,0:T(8,128)(2,1)} %param.9) | copy-start | bytes 6291460
  6.5 38.2 %all-gather.16.cloned.1.call-start = ((), (), s32[]{:S(2)}) async-start(), calls=%async_computation.5 | async-start | bytes 3145728 | tf_op jit(solution)/shard_map/all_gather | solution.py:47
  7.3 92.1 %all-gather.18.cloned.1.call-start = ((), (), s32[]{:S(2)}) async-start(), calls=%async_computation.6 | async-start | bytes 4456448 | tf_op jit(solution)/shard_map/all_gather | solution.py:57
  8.0 124.3 %all-gather.14.cloned.1.call-start = ((), (), s32[]{:S(2)}) async-start(), calls=%async_computation.3 | async-start | bytes 3145728 | tf_op jit(solution)/shard_map/all_gather | solution.py:46
  8.7 158.0 %all-gather.20.cloned.1.call-start = ((), (), s32[]{:S(2)}) async-start(), calls=%async_computation.7 | async-start | bytes 3145728 | tf_op jit(solution)/shard_map/all_gather | solution.py:66
  105.4 28.9 %copy-start.5 = (f32[2048]{0:T(1024)S(1)}, f32[2048]{0:T(1024)}, u32[]{:S(2)}) copy-start(f32[2048]{0:T(1024)} %param.8) | copy-start | bytes 24580
  107.5 166.7 %reduce-scatter.4.cloned.1.call-start = ((), (), s32[]{:S(2)}) async-start(), calls=%async_computation.4 | async-start | bytes 8912896 | tf_op jit(solution)/shard_map/reduce_scatter | solution.py:82
  136.5 1.3 copy-start.3
  143.7 237.5 %reduce-scatter.6.cloned.1.call-start = ((), (), s32[]{:S(2)}) async-start(), calls=%async_computation.8 | async-start | bytes 8912896 | tf_op jit(solution)/shard_map/reduce_scatter | solution.py:83
  174.0 285.5 %all-gather.22.cloned.1.call-start = ((), (), s32[]{:S(2)}) async-start(), calls=%async_computation.9 | async-start | bytes 3145728 | tf_op jit(solution)/shard_map/all_gather | solution.py:22
  426.6 161.5 %all-gather.24.cloned.1.call-start = ((), (), s32[]{:S(2)}) async-start(), calls=%async_computation.10 | async-start | bytes 17825792 | tf_op jit(solution)/shard_map/all_gather | solution.py:97
  427.4 266.4 %reduce-scatter.8.cloned.1.call-start = ((), (), s32[]{:S(2)}) async-start(), calls=%async_computation.13 | async-start | bytes 8912896 | tf_op jit(solution)/shard_map/reduce_scatter | solution.py:84
  435.2 292.8 %copy-start.2 = (f32[2,128,1024]{2,1,0:T(8,128)S(1)}, f32[2,128,1024]{2,1,0:T(8,128)}, u32[]{:S(2)}) copy-start(f32[2,128,1024]{2,1,0:T(8,128)} %get-tuple-element.11) | copy-start | bytes 3145732
  435.2 292.8 %all-gather.26.cloned.1.call-start = ((), (), s32[]{:S(2)}) async-start(), calls=%async_computation.11 | async-start | bytes 3145728 | tf_op jit(solution)/shard_map/all_gather | solution.py:22
  602.5 202.0 %all-gather.32.cloned.1.call-start = ((), (), s32[]{:S(2)}) async-start(), calls=%async_computation.15 | async-start | bytes 8912896 | tf_op jit(solution)/shard_map/all_gather | solution.py:29
  693.9 131.9 %all-gather.28.cloned.1.call-start = ((), (), s32[]{:S(2)}) async-start(), calls=%async_computation.12 | async-start | bytes 1572864 | tf_op jit(solution)/shard_map/all_gather | solution.py:22
  742.8 189.9 %copy-start.4 = (f32[128,1024]{1,0:T(8,128)S(1)}, f32[128,1024]{1,0:T(8,128)}, u32[]{:S(2)}) copy-start(f32[128,1024]{1,0:T(8,128)} %reduce-scatter.8.cloned.1.call-done) | copy-start | bytes 1572868
  742.9 113.6 %all-gather.34.cloned.1.call-start = ((), (), s32[]{:S(2)}) async-start(), calls=%async_computation.16 | async-start | bytes 1572864 | tf_op jit(solution)/shard_map/all_gather | solution.py:22
  835.0 97.8 %all-gather.30.cloned.1.call-start = ((), (), s32[]{:S(2)}) async-start(), calls=%async_computation.14 | async-start | bytes 8912896 | tf_op jit(solution)/shard_map/all_gather | solution.py:29
  835.6 146.0 %copy-start.1 = (bf16[2,8,256,256]{3,2,1,0:T(8,128)(2,1)S(1)}, bf16[2,8,256,256]{3,2,1,0:T(8,128)(2,1)}, u32[]{:S(2)}) copy-start(bf16[2,8,256,256]{3,2,1,0:T(8,128)(2,1)} %param.9) | copy-start | bytes 6291460
Sparse Core Ops, SparseCore 0:
  8.9 35.8 all-gather.15
  46.9 52.4 all-gather.17
  100.9 31.2 all-gather.13
  133.7 33.0 all-gather.19
  170.7 103.4 reduce-scatter.3
  278.1 103.0 reduce-scatter.5
  426.8 32.6 all-gather.21
  461.6 126.4 all-gather.23
  592.2 101.6 reduce-scatter.7
  695.2 32.7 all-gather.25
  730.2 74.2 all-gather.31
  805.9 19.8 all-gather.27
  835.1 21.2 all-gather.33
  858.4 74.2 all-gather.29
where the time goes:
time: 989 us; the launch traced here: 988 us
  waiting for transfers between devices  804 us (81%)
  blocking collectives  79.6 us (8%)
  matrix products  71.7 us (7%)
  between operations  14.1 us (1%)
  other arithmetic  11.6 us (1%)
    all_gather x2, waiting for transfers between devices, panel_product(): lax.all_gather(right_block, 'dp', axis=1, tiled=True)  138 us
    all_gather x1, waiting for transfers between devices, per_device(): columns = lax.all_gather(iterate, 'dp', axis=1, tiled=True)  129 us
    reduce_scatter x1, waiting for transfers between devices, per_device(): lax.psum_scatter(g_part, 'dp', scatter_dimension=0, tiled=True)  107 us
    all_gather x4, waiting for transfers between devices, panel_rows(): return lax.all_gather(block, 'fac', axis=2, tiled=True)  100 us
    reduce_scatter x1, waiting for transfers between devices, per_device(): lax.psum_scatter(a_part, 'dp', scatter_dimension=0, tiled=True)  100 us
    reduce_scatter x1, waiting for transfers between devices, per_device(): lax.psum_scatter(grad_part, 'dp', scatter_dimension=0, tiled=True)  91.3 us
    all_gather x1, waiting for transfers between devices, per_device(): lax.all_gather(w_out, 'dp', axis=1, tiled=True)  54.7 us
    psum x1, blocking collectives, per_device(): lax.psum((jnp.sum(a_block * a_block), jnp.sum(g_block * g_block)), ('dp',...  40.5 us
  transfers between devices with their start and end apart: 14, of which 14 were waited for; matrix products, arithmetic and copies ran while one was open for 7% of the time, Pallas kernels for 0%

commit v1 on v0

--- a/solution.py
+++ b/solution.py
@@ -9,6 +9,22 @@
 epsilon = 1e-06
 highest = lax.Precision.HIGHEST
 contract_first = (((0,), (0,)), ((), ()))
+
+
+def ring_product(value, axis, dim, term):
+    size, index, span = (lax.axis_size(axis), lax.axis_index(axis), value.shape[dim])
+    upward = [(i, (i + 1) % size) for i in range(size)]
+    left = [(i, (i - 1) % size) for i in range(size)]
+    middle = size // 2
+    from_left = from_right = value
+    total = term(value, index * span)
+    for step in range(1, middle + 1):
+        from_left = lax.ppermute(from_left, axis, upward)
+        if step < size - middle:
+            from_right = lax.ppermute(from_right, axis, left)
+            total = total + term(from_right, (index + step) % size * span)
+        total = total + term(from_left, (index - step) % size * span)
+    return total
 
 
 def keep_mask(occupations):
@@ -23,11 +39,16 @@
 
 
 def panel_product(left_rows, right_block):
-    return jnp.einsum(
-        "brk,bkc->brc",
-        left_rows,
-        lax.all_gather(right_block, "dp", axis=1, tiled=True),
-        precision=highest,
+    return ring_product(
+        right_block,
+        "dp",
+        1,
+        lambda shard, at: jnp.einsum(
+            "brk,bkc->brc",
+            lax.dynamic_slice_in_dim(left_rows, at, shard.shape[1], axis=2),
+            shard,
+            precision=highest,
+        ),
     )
 
 

time: 989 us -> 923 us (0.933)
  waiting for transfers between devices: 804 us -> 602 us
  starting transfers between devices: 0.93 us -> 104 us
  matrix products: 71.7 us -> 91.1 us
    all_gather x2 -> x0, waiting for transfers between devices: 138 us -> none  [panel_product(): lax.all_gather(right_block, 'dp', axis=1, tiled=True)]
    ppermute x0 -> x30, starting transfers between devices: none -> 104 us  [the longest x16 58.7 us: ring_product(): from_left = lax.ppermute(from_left, axis, upward)]
    all_gather x4, waiting for transfers between devices: 100 us -> 32.1 us  [panel_rows(): return lax.all_gather(block, 'fac', axis=2, tiled=True)]
    ppermute x0 -> x30, waiting for transfers between devices: none -> 39.9 us  [the longest x16 31.1 us: ring_product(): from_left = lax.ppermute(from_left, axis, upward)]
    reduce_scatter x1, waiting for transfers between devices: 91.3 us -> 60.6 us  [per_device(): lax.psum_scatter(grad_part, 'dp', scatter_dimension=0, tiled=True)]
    dot_general x2 -> x32, matrix products: 17.3 us -> 36.3 us  [panel_product(): jnp.einsum('brk,bkc->brc', lax.dynamic_slice_in_dim(left_rows, at, shard....]
  transfers between devices with their start and end apart: 14 -> 42, of which waited for: 14 -> 20; matrix products, arithmetic and copies ran while one was open for 7% -> 11% of each run, Pallas kernels for 0% -> 0%
where the time goes in v1:
time: 923 us; the launch traced here: 914 us
  waiting for transfers between devices  602 us (65%)
  starting transfers between devices  104 us (11%)
  matrix products  91.1 us (10%)
  blocking collectives  86.7 us (9%)
  between operations  15.3 us (2%)
  other arithmetic  9.61 us (1%)
    all_gather x1, waiting for transfers between devices, per_device(): columns = lax.all_gather(iterate, 'dp', axis=1, tiled=True)  129 us
    reduce_scatter x1, waiting for transfers between devices, per_device(): lax.psum_scatter(g_part, 'dp', scatter_dimension=0, tiled=True)  107 us
    reduce_scatter x1, waiting for transfers between devices, per_device(): lax.psum_scatter(a_part, 'dp', scatter_dimension=0, tiled=True)  92 us
    reduce_scatter x1, waiting for transfers between devices, per_device(): lax.psum_scatter(grad_part, 'dp', scatter_dimension=0, tiled=True)  60.6 us
    ppermute x16, starting transfers between devices, ring_product(): from_left = lax.ppermute(from_left, axis, upward)  58.7 us
    all_gather x1, waiting for transfers between devices, per_device(): lax.all_gather(w_out, 'dp', axis=1, tiled=True)  54.7 us
    psum x1, blocking collectives, per_device(): inner_sum = lax.psum(jnp.sum(grad_block * pre), ('dp', 'fac'))  45.8 us
    ppermute x14, starting transfers between devices, ring_product(): from_right = lax.ppermute(from_right, axis, left)  44.9 us
  transfers between devices with their start and end apart: 42, of which 20 were waited for; matrix products, arithmetic and copies ran while one was open for 11% of the time, Pallas kernels for 0%

profile of v1, /device:TPU:0, one launch (start us, length us, event | category | flops | bytes accessed | tf_op | source)
XLA Modules:
  0.0 913.5 jit_solution(18093133252359987454)
XLA Ops:
  9.9 34.8 %all-gather.13.cloned.1.call-done = bf16[512,2048]{1,0:T(8,128)(2,1)} async-done(((bf16[512,1024]{1,0:T(8,128)(2,1)}), bf16[512,2048]{1,0:T(8,128)(2,1)}) %all-gather.13.cloned.1.call-update) | async-done | bytes 2097168 | tf_op jit(solution)/shard_map/all_gather | solution.py:68
  44.7 54.7 %all-gather.15.cloned.1.call-done = bf16[1024,2048]{1,0:T(8,128)(2,1)} async-done(((bf16[1024,128]{1,0:T(8,128)(2,1)}), bf16[1024,2048]{1,0:T(8,128)(2,1)}) %all-gather.15.cloned.1.call-update) | async-done | bytes 4194320 | tf_op jit(solution)/shard_map/all_gather | solution.py:78
  99.4 5.2 fusion.9
  107.5 24.8 %all-gather.11.cloned.1.call-done = bf16[512,2048]{1,0:T(8,128)(2,1)} async-done(((bf16[512,1024]{1,0:T(8,128)(2,1)}), bf16[512,2048]{1,0:T(8,128)(2,1)}) %all-gather.11.cloned.1.call-update) | async-done | bytes 2097168 | tf_op jit(solution)/shard_map/all_gather | solution.py:67
  136.4 6.0 convolution_multiply_fusion.2
  142.4 24.4 %all-gather.17.cloned.1.call-done = bf16[512,2048]{1,0:T(8,128)(2,1)} async-done(((bf16[512,1024]{1,0:T(8,128)(2,1)}), bf16[512,2048]{1,0:T(8,128)(2,1)}) %all-gather.17.cloned.1.call-update) | async-done | bytes 2097168 | tf_op jit(solution)/shard_map/all_gather | solution.py:87
  166.8 7.3 convolution_multiply_fusion.1
  174.1 7.7 convolution_multiply_fusion
  182.2 92.0 %reduce-scatter.4.cloned.1.call-done = f32[128,1024]{1,0:T(8,128)} async-done(((f32[2048,1024]{1,0:T(8,128)}), f32[128,1024]{1,0:T(8,128)}) %reduce-scatter.4.cloned.1.call-update) | async-done | bytes 524304 | tf_op jit(solution)/shard_map/reduce_scatter | solution.py:103
  274.2 107.0 %reduce-scatter.6.cloned.1.call-done = f32[128,1024]{1,0:T(8,128)} async-done(((f32[2048,1024]{1,0:T(8,128)}), f32[128,1024]{1,0:T(8,128)}) %reduce-scatter.6.cloned.1.call-update) | async-done | bytes 524304 | tf_op jit(solution)/shard_map/reduce_scatter | solution.py:104
  383.3 40.8 %all-reduce = (f32[1]{0:T(128)}, f32[1]{0:T(128)}) all-reduce(f32[1]{0:T(128)} %bitcast.2, f32[1]{0:T(128)} %bitcast), channel_id=1, replica_groups=mesh['dp'=16,'fac'=2] {'dp','fac'}, use_global_device_ids=true, to_apply=%region_8.9 | all-reduce | flops 2 | bytes 16 | tf_op jit(solution)/shard_map/psum | solution.py:112
  427.8 60.6 %reduce-scatter.8.cloned.1.call-done = f32[128,1024]{1,0:T(8,128)} async-done(((f32[2048,1024]{1,0:T(8,128)}), f32[128,1024]{1,0:T(8,128)}) %reduce-scatter.8.cloned.1.call-update) | async-done | bytes 524304 | tf_op jit(solution)/shard_map/reduce_scatter | solution.py:105
  492.9 7.2 collective-permute-done.1
  502.0 20.7 %all-gather.19.cloned.1.call-done = f32[2,128,2048]{2,1,0:T(8,128)} async-done(((f32[2,128,1024]{2,1,0:T(8,128)}), f32[2,128,2048]{2,1,0:T(8,128)}) %all-gather.19.cloned.1.call-update) | async-done | bytes 2097168 | tf_op jit(solution)/shard_map/all_gather | solution.py:38
  522.7 128.7 %all-gather.21.cloned.1.call-done = f32[2,2048,1024]{2,1,0:T(8,128)} async-done(((f32[2,128,1024]{2,1,0:T(8,128)}), f32[2,2048,1024]{2,1,0:T(8,128)}) %all-gather.21.cloned.1.call-update) | async-done | bytes 16777232 | tf_op jit(solution)/shard_map/all_gather | solution.py:118
  651.4 14.4 %fusion.161 = f32[2,128,1024]{2,1,0:T(8,128)} fusion(f32[2,128,2048]{2,1,0:T(8,128)} %all-gather.19.cloned.1.call-done, f32[2,2048,1024]{2,1,0:T(8,128)} %all-gather.21.cloned.1.call-done), kind=kOutput, calls=%fused_computation.201 | convolution fusion | flops 6442450944 | bytes 19922944 | tf_op jit(solution)/shard_map/brk,bkc->brc/dot_general | solution.py:119
  667.1 6.7 collective-permute-done.2
  673.8 4.7 collective-permute-start.4
  678.5 6.7 collective-permute-start.7
  685.3 4.6 collective-permute-start.6
  690.0 8.9 collective-permute-start.9
  701.5 9.7 %collective-permute-start.11 = (f32[1,128,1024]{2,1,0:T(8,128)}, f32[1,128,1024]{2,1,0:T(8,128)}, u32[]{:S(2)}, u32[]{:S(2)}) collective-permute-start(f32[1,128,1024]{2,1,0:T(8,128)} %collective-permute-done.9), channel_id=1, source_target_pairs={{0,2},{2,4},{4,6},{6,8},{8,10},{10,12},{12,14},{14,16},{16,18},{18... | collective-permute-start | bytes 1572872 | tf_op jit(solution)/shard_map/ppermute | solution.py:22
  711.2 13.7 %convolution_subtract_fusion = f32[2,128,1024]{2,1,0:T(8,128)S(1)} fusion(f32[2,128,2048]{2,1,0:T(8,128)} %all-gather.23.cloned.1.call-done, f32[2,2048,1024]{2,1,0:T(8,128)} %all-gather.21.cloned.1.call-done, f32[2,128,1024]{2,1,0:T(8,128)S(1)} %copy-done.2), kind=kOutput, calls=%fused_computation.14 | convolution fusion | flops 6442975232 | bytes 20971520 | tf_op jit(solution)/shard_map/brk,bkc->brc/dot_general | solution.py:120
  733.3 4.6 collective-permute-start.12
  737.9 16.6 %collective-permute-start.14 = (f32[1,128,1024]{2,1,0:T(8,128)}, f32[1,128,1024]{2,1,0:T(8,128)}, u32[]{:S(2)}, u32[]{:S(2)}) collective-permute-start(f32[1,128,1024]{2,1,0:T(8,128)} %collective-permute-done.13), channel_id=1, source_target_pairs={{0,2},{2,4},{4,6},{6,8},{8,10},{10,12},{12,14},{14,16},{16,18},{18... | collective-permute-start | bytes 1572872 | tf_op jit(solution)/shard_map/ppermute | solution.py:22
  782.8 7.3 collective-permute-done.20
  794.5 11.4 %all-gather.27.cloned.1.call-done = f32[128,2048]{1,0:T(8,128)} async-done(((f32[128,1024]{1,0:T(8,128)}), f32[128,2048]{1,0:T(8,128)}) %all-gather.27.cloned.1.call-update) | async-done | bytes 1048592 | tf_op jit(solution)/shard_map/all_gather | solution.py:38
  813.5 4.5 collective-permute-start.23
  824.7 4.7 collective-permute-start.25
  836.1 4.7 collective-permute-start.27
  850.0 7.7 collective-permute-done.29
  858.9 45.8 %psum.23 = f32[]{:T(128)} all-reduce(f32[]{:T(128)} %get-tuple-element.15), channel_id=1, replica_groups=mesh['dp'=16,'fac'=2] {'dp','fac'}, use_global_device_ids=true, to_apply=%region_11.12 | all-reduce | flops 1 | bytes 8 | tf_op jit(solution)/shard_map/psum | solution.py:125
  (172 shorter events, 99.9 us)
Async XLA Ops:
  6.5 38.2 %all-gather.13.cloned.1.call-start = ((), (), s32[]{:S(2)}) async-start(), calls=%async_computation.5 | async-start | bytes 3145728 | tf_op jit(solution)/shard_map/all_gather | solution.py:68
  7.3 92.1 %all-gather.15.cloned.1.call-start = ((), (), s32[]{:S(2)}) async-start(), calls=%async_computation.6 | async-start | bytes 4456448 | tf_op jit(solution)/shard_map/all_gather | solution.py:78
  8.0 124.2 %all-gather.11.cloned.1.call-start = ((), (), s32[]{:S(2)}) async-start(), calls=%async_computation.3 | async-start | bytes 3145728 | tf_op jit(solution)/shard_map/all_gather | solution.py:67
  8.7 158.0 %all-gather.17.cloned.1.call-start = ((), (), s32[]{:S(2)}) async-start(), calls=%async_computation.7 | async-start | bytes 3145728 | tf_op jit(solution)/shard_map/all_gather | solution.py:87
  107.5 166.7 %reduce-scatter.4.cloned.1.call-start = ((), (), s32[]{:S(2)}) async-start(), calls=%async_computation.4 | async-start | bytes 8912896 | tf_op jit(solution)/shard_map/reduce_scatter | solution.py:103
  142.4 238.8 %reduce-scatter.6.cloned.1.call-start = ((), (), s32[]{:S(2)}) async-start(), calls=%async_computation.8 | async-start | bytes 8912896 | tf_op jit(solution)/shard_map/reduce_scatter | solution.py:104
  174.1 314.3 %reduce-scatter.8.cloned.1.call-start = ((), (), s32[]{:S(2)}) async-start(), calls=%async_computation.13 | async-start | bytes 8912896 | tf_op jit(solution)/shard_map/reduce_scatter | solution.py:105
  181.9 340.8 %all-gather.19.cloned.1.call-start = ((), (), s32[]{:S(2)}) async-start(), calls=%async_computation.9 | async-start | bytes 3145728 | tf_op jit(solution)/shard_map/all_gather | solution.py:38
  427.1 224.3 %all-gather.21.cloned.1.call-start = ((), (), s32[]{:S(2)}) async-start(), calls=%async_computation.10 | async-start | bytes 17825792 | tf_op jit(solution)/shard_map/all_gather | solution.py:118
  427.8 283.4 %all-gather.23.cloned.1.call-start = ((), (), s32[]{:S(2)}) async-start(), calls=%async_computation.11 | async-start | bytes 3145728 | tf_op jit(solution)/shard_map/all_gather | solution.py:38
  488.4 11.6 %collective-permute-start.1 = (f32[1,128,1024]{2,1,0:T(8,128)}, f32[1,128,1024]{2,1,0:T(8,128)S(1)}, u32[]{:S(2)}, u32[]{:S(2)}) collective-permute-start(f32[1,128,1024]{2,1,0:T(8,128)} %bitcast.192), channel_id=1, source_target_pairs={{0,2},{2,4},{4,6},{6,8},{8,10},{10,12},{12,14},{14,16},{16,18},{18... | collective-permute-start | bytes 1572872 | tf_op jit(solution)/shard_map/ppermute | solution.py:22
  488.4 177.4 %collective-permute-start = (f32[1,128,1024]{2,1,0:T(8,128)}, f32[1,128,1024]{2,1,0:T(8,128)S(1)}, u32[]{:S(2)}, u32[]{:S(2)}) collective-permute-start(f32[1,128,1024]{2,1,0:T(8,128)} %bitcast.193), channel_id=1, source_target_pairs={{0,30},{2,0},{4,2},{6,4},{8,6},{10,8},{12,10},{14,12},{16,14},{18,... | collective-permute-start | bytes 1572872 | tf_op jit(solution)/shard_map/ppermute | solution.py:24
  500.0 167.1 %collective-permute-start.3 = (f32[1,128,1024]{2,1,0:T(8,128)S(1)}, f32[1,128,1024]{2,1,0:T(8,128)S(1)}, u32[]{:S(2)}, u32[]{:S(2)}) collective-permute-start(f32[1,128,1024]{2,1,0:T(8,128)S(1)} %collective-permute-done.1), channel_id=1, source_target_pairs={{0,2},{2,4},{4,6},{6,8},{8,10},{10,12},{12,14},{14,16},{16,18},{18... | collective-permute-start | bytes 1572872 | tf_op jit(solution)/shard_map/ppermute | solution.py:22
  665.8 93.4 %all-gather.25.cloned.1.call-start = ((), (), s32[]{:S(2)}) async-start(), calls=%async_computation.12 | async-start | bytes 1572864 | tf_op jit(solution)/shard_map/all_gather | solution.py:38
  685.3 13.6 %collective-permute-start.6 = (f32[1,128,1024]{2,1,0:T(8,128)S(1)}, f32[1,128,1024]{2,1,0:T(8,128)S(1)}, u32[]{:S(2)}, u32[]{:S(2)}) collective-permute-start(f32[1,128,1024]{2,1,0:T(8,128)S(1)} %collective-permute-done.4), channel_id=1, source_target_pairs={{0,30},{2,0},{4,2},{6,4},{8,6},{10,8},{12,10},{14,12},{16,14},{18,... | collective-permute-start | bytes 1572872 | tf_op jit(solution)/shard_map/ppermute | solution.py:24
  690.0 11.5 %collective-permute-start.9 = (f32[1,128,1024]{2,1,0:T(8,128)S(1)}, f32[1,128,1024]{2,1,0:T(8,128)}, u32[]{:S(2)}, u32[]{:S(2)}) collective-permute-start(f32[1,128,1024]{2,1,0:T(8,128)S(1)} %collective-permute-done.7), channel_id=1, source_target_pairs={{0,2},{2,4},{4,6},{6,8},{8,10},{10,12},{12,14},{14,16},{16,18},{18... | collective-permute-start | bytes 1572872 | tf_op jit(solution)/shard_map/ppermute | solution.py:22
  698.9 27.2 %collective-permute-start.8 = (f32[1,128,1024]{2,1,0:T(8,128)S(1)}, f32[1,128,1024]{2,1,0:T(8,128)}, u32[]{:S(2)}, u32[]{:S(2)}) collective-permute-start(f32[1,128,1024]{2,1,0:T(8,128)S(1)} %collective-permute-done.6), channel_id=1, source_target_pairs={{0,30},{2,0},{4,2},{6,4},{8,6},{10,8},{12,10},{14,12},{16,14},{18,... | collective-permute-start | bytes 1572872 | tf_op jit(solution)/shard_map/ppermute | solution.py:24
  701.5 24.7 %collective-permute-start.11 = (f32[1,128,1024]{2,1,0:T(8,128)}, f32[1,128,1024]{2,1,0:T(8,128)}, u32[]{:S(2)}, u32[]{:S(2)}) collective-permute-start(f32[1,128,1024]{2,1,0:T(8,128)} %collective-permute-done.9), channel_id=1, source_target_pairs={{0,2},{2,4},{4,6},{6,8},{8,10},{10,12},{12,14},{14,16},{16,18},{18... | collective-permute-start | bytes 1572872 | tf_op jit(solution)/shard_map/ppermute | solution.py:22
  726.0 79.9 %all-gather.27.cloned.1.call-start = ((), (), s32[]{:S(2)}) async-start(), calls=%async_computation.14 | async-start | bytes 1572864 | tf_op jit(solution)/shard_map/all_gather | solution.py:38
  726.2 11.8 %collective-permute-start.13 = (f32[1,128,1024]{2,1,0:T(8,128)}, f32[1,128,1024]{2,1,0:T(8,128)}, u32[]{:S(2)}, u32[]{:S(2)}) collective-permute-start(f32[1,128,1024]{2,1,0:T(8,128)} %collective-permute-done.11), channel_id=1, source_target_pairs={{0,2},{2,4},{4,6},{6,8},{8,10},{10,12},{12,14},{14,16},{16,18},{18... | collective-permute-start | bytes 1572872 | tf_op jit(solution)/shard_map/ppermute | solution.py:22
  728.8 25.7 %collective-permute-start.16 = (f32[1,128,1024]{2,1,0:T(8,128)}, f32[1,128,1024]{2,1,0:T(8,128)}, u32[]{:S(2)}, u32[]{:S(2)}) collective-permute-start(f32[1,128,1024]{2,1,0:T(8,128)} %get-tuple-element.10), channel_id=1, source_target_pairs={{0,2},{2,4},{4,6},{6,8},{8,10},{10,12},{12,14},{14,16},{16,18},{18... | collective-permute-start | bytes 1572872 | tf_op jit(solution)/shard_map/ppermute | solution.py:22
  730.5 27.0 %collective-permute-start.15 = (f32[1,128,1024]{2,1,0:T(8,128)}, f32[1,128,1024]{2,1,0:T(8,128)}, u32[]{:S(2)}, u32[]{:S(2)}) collective-permute-start(f32[1,128,1024]{2,1,0:T(8,128)} %get-tuple-element.10), channel_id=1, source_target_pairs={{0,30},{2,0},{4,2},{6,4},{8,6},{10,8},{12,10},{14,12},{16,14},{18,... | collective-permute-start | bytes 1572872 | tf_op jit(solution)/shard_map/ppermute | solution.py:24
  733.3 40.9 %collective-permute-start.12 = (f32[1,128,1024]{2,1,0:T(8,128)}, f32[1,128,1024]{2,1,0:T(8,128)}, u32[]{:S(2)}, u32[]{:S(2)}) collective-permute-start(f32[1,128,1024]{2,1,0:T(8,128)} %collective-permute-done.10), channel_id=1, source_target_pairs={{0,30},{2,0},{4,2},{6,4},{8,6},{10,8},{12,10},{14,12},{16,14},{18,... | collective-permute-start | bytes 1572872 | tf_op jit(solution)/shard_map/ppermute | solution.py:24
  737.9 37.9 %collective-permute-start.14 = (f32[1,128,1024]{2,1,0:T(8,128)}, f32[1,128,1024]{2,1,0:T(8,128)}, u32[]{:S(2)}, u32[]{:S(2)}) collective-permute-start(f32[1,128,1024]{2,1,0:T(8,128)} %collective-permute-done.13), channel_id=1, source_target_pairs={{0,2},{2,4},{4,6},{6,8},{8,10},{10,12},{12,14},{14,16},{16,18},{18... | collective-permute-start | bytes 1572872 | tf_op jit(solution)/shard_map/ppermute | solution.py:22
  754.5 23.8 %collective-permute-start.18 = (f32[1,128,1024]{2,1,0:T(8,128)}, f32[1,128,1024]{2,1,0:T(8,128)}, u32[]{:S(2)}, u32[]{:S(2)}) collective-permute-start(f32[1,128,1024]{2,1,0:T(8,128)} %collective-permute-done.16), channel_id=1, source_target_pairs={{0,2},{2,4},{4,6},{6,8},{8,10},{10,12},{12,14},{14,16},{16,18},{18... | collective-permute-start | bytes 1572872 | tf_op jit(solution)/shard_map/ppermute | solution.py:22
  757.5 22.1 %collective-permute-start.17 = (f32[1,128,1024]{2,1,0:T(8,128)}, f32[1,128,1024]{2,1,0:T(8,128)}, u32[]{:S(2)}, u32[]{:S(2)}) collective-permute-start(f32[1,128,1024]{2,1,0:T(8,128)} %collective-permute-done.15), channel_id=1, source_target_pairs={{0,30},{2,0},{4,2},{6,4},{8,6},{10,8},{12,10},{14,12},{16,14},{18,... | collective-permute-start | bytes 1572872 | tf_op jit(solution)/shard_map/ppermute | solution.py:24
  778.3 11.8 %collective-permute-start.20 = (f32[1,128,1024]{2,1,0:T(8,128)}, f32[1,128,1024]{2,1,0:T(8,128)}, u32[]{:S(2)}, u32[]{:S(2)}) collective-permute-start(f32[1,128,1024]{2,1,0:T(8,128)} %collective-permute-done.18), channel_id=1, source_target_pairs={{0,2},{2,4},{4,6},{6,8},{8,10},{10,12},{12,14},{14,16},{16,18},{18... | collective-permute-start | bytes 1572872 | tf_op jit(solution)/shard_map/ppermute | solution.py:22
  779.6 13.8 %collective-permute-start.19 = (f32[1,128,1024]{2,1,0:T(8,128)}, f32[1,128,1024]{2,1,0:T(8,128)}, u32[]{:S(2)}, u32[]{:S(2)}) collective-permute-start(f32[1,128,1024]{2,1,0:T(8,128)} %collective-permute-done.17), channel_id=1, source_target_pairs={{0,30},{2,0},{4,2},{6,4},{8,6},{10,8},{12,10},{14,12},{16,14},{18,... | collective-permute-start | bytes 1572872 | tf_op jit(solution)/shard_map/ppermute | solution.py:24
  790.1 19.9 %collective-permute-start.22 = (f32[1,128,1024]{2,1,0:T(8,128)}, f32[1,128,1024]{2,1,0:T(8,128)}, u32[]{:S(2)}, u32[]{:S(2)}) collective-permute-start(f32[1,128,1024]{2,1,0:T(8,128)} %collective-permute-done.20), channel_id=1, source_target_pairs={{0,2},{2,4},{4,6},{6,8},{8,10},{10,12},{12,14},{14,16},{16,18},{18... | collective-permute-start | bytes 1572872 | tf_op jit(solution)/shard_map/ppermute | solution.py:22
  793.3 20.2 %collective-permute-start.21 = (f32[1,128,1024]{2,1,0:T(8,128)}, f32[1,128,1024]{2,1,0:T(8,128)S(1)}, u32[]{:S(2)}, u32[]{:S(2)}) collective-permute-start(f32[1,128,1024]{2,1,0:T(8,128)} %collective-permute-done.19), channel_id=1, source_target_pairs={{0,30},{2,0},{4,2},{6,4},{8,6},{10,8},{12,10},{14,12},{16,14},{18,... | collective-permute-start | bytes 1572872 | tf_op jit(solution)/shard_map/ppermute | solution.py:24
  809.9 13.6 %collective-permute-start.24 = (f32[1,128,1024]{2,1,0:T(8,128)}, f32[1,128,1024]{2,1,0:T(8,128)S(1)}, u32[]{:S(2)}, u32[]{:S(2)}) collective-permute-start(f32[1,128,1024]{2,1,0:T(8,128)} %collective-permute-done.22), channel_id=1, source_target_pairs={{0,2},{2,4},{4,6},{6,8},{8,10},{10,12},{12,14},{14,16},{16,18},{18... | collective-permute-start | bytes 1572872 | tf_op jit(solution)/shard_map/ppermute | solution.py:22
  836.1 13.3 %collective-permute-start.27 = (f32[1,128,1024]{2,1,0:T(8,128)S(1)}, f32[1,128,1024]{2,1,0:T(8,128)S(1)}, u32[]{:S(2)}, u32[]{:S(2)}) collective-permute-start(f32[1,128,1024]{2,1,0:T(8,128)S(1)} %collective-permute-done.25), channel_id=1, source_target_pairs={{0,30},{2,0},{4,2},{6,4},{8,6},{10,8},{12,10},{14,12},{16,14},{18,... | collective-permute-start | bytes 1572872 | tf_op jit(solution)/shard_map/ppermute | solution.py:24
  (33 other events, 901.1 us)
Sparse Core Ops, SparseCore 0:
  8.9 35.8 all-gather.12
  46.9 52.4 all-gather.14
  101.0 31.2 all-gather.10
  133.7 33.0 all-gather.16
  170.7 103.4 reduce-scatter.3
  278.1 103.0 reduce-scatter.5
  385.3 103.0 reduce-scatter.7
  490.0 32.7 all-gather.18
  524.9 126.4 all-gather.20
  665.9 31.2 all-gather.22
  726.1 23.6 all-gather.24
  778.4 27.4 all-gather.26
